TPU v7x, 32 devices: a whole 2x2x4 slice. The times are simulated.
32 devices in a mesh: ctx: 16 (over z, x, core), vocab: 2 (over y).
Axes of the slice: x: 2, y: 2, z: 4, core: 2. Of those that a mesh axis runs over, the one named last changes fastest.
Arguments:
- hidden: bfloat16 [4096, 8192], P('ctx', 'vocab'), may hold values from -540 to 540
- norm_gain: float32 [8192], P('vocab'), may hold values from 0.5 to 1.5
- head: bfloat16 [15808, 8192], P('ctx', 'vocab'), may hold values from -0.53033009 to 0.53033009
- masked_pos: int32 [2, 16], replicated, may hold values from 0 to 2047, as said below
- masked_targets: int32 [2, 16], replicated, may hold values from 0 to 15807
- t_num: int32 [2], replicated, may hold values from 1 to 3, as said below
- t_den: int32 [2], replicated, may hold values from 192 to 319
Outputs:
- loss_value: float32 [], replicated
- grad_hidden: bfloat16 [4096, 8192], P('ctx', 'vocab')
- grad_head: bfloat16 [15808, 8192], P('ctx', 'vocab')
- grad_gain: float32 [8192], P('vocab')
Inputs may be any that keep to these rules, and one draw needn't show every extreme that they name: `masked_pos`: each row lists 16 distinct positions of one sequence in increasing order; at most 8 of them fall in one aligned block of 256 positions, and exactly 8 in some blocks of every sequence. `t_num`: the two numerators differ.
All inputs are finite; a program needn't handle non-finite values.
Results may differ from a plain program's by a relative error of at most 0.0081.
Values may be sent and summed in bfloat16 or wider, within the bound.
No kernel may reach another device: no remote copies, remote signals or barrier semaphores. Data moves between devices by JAX's collectives and lax.ppermute only.
A program may use at most 64 MiB of HBM per device.

v0:
```python
import jax
import jax.numpy as jnp
from jax import lax
from jax.sharding import PartitionSpec as P

CAP = 8
EPSILON = 1e-05
LOSS_SCALE = 1024.0


def joined(part, axis, combine):
    gathered = jax.tree.map(lambda a: lax.all_gather(a, axis), part)

    def take(source):
        return jax.tree.map(lambda a: lax.dynamic_index_in_dim(a, source, 0, False), gathered)

    return lax.fori_loop(
        1, lax.axis_size(axis), lambda source, state: combine(state, take(source)), take(0)
    )


def contract_last(left, right):
    return lax.dot_general(
        left, right, (((1,), (1,)), ((), ())), preferred_element_type=jnp.float32
    )


def combine_stats(first, second):
    row_top = jnp.maximum(first[0], second[0])
    exp_total = first[1] * jnp.exp(first[0] - row_top) + second[1] * jnp.exp(second[0] - row_top)
    return (row_top, exp_total, first[2] + second[2])


def on_device(hidden, norm_gain, head, masked_pos, masked_targets, t_num, t_den):
    tok_here, width_here = hidden.shape
    voc_here = head.shape[0]
    ctx_count = lax.axis_size("ctx")
    vocab_count = lax.axis_size("vocab")
    ctx_index = lax.axis_index("ctx")
    vocab_index = lax.axis_index("vocab")
    blocks = ctx_count // 2
    slot_count = masked_pos.shape[1]
    model_width = width_here * vocab_count
    seq_here = ctx_index // blocks
    block_here = ctx_index % blocks
    block_of = masked_pos // tok_here
    block_ids = jnp.arange(blocks, dtype=jnp.int32)
    counts = jnp.sum((block_of[:, :, None] == block_ids[None, None, :]).astype(jnp.int32), axis=1)
    offsets = jnp.cumsum(counts, axis=1) - counts
    weight = t_den.astype(jnp.float32) / (t_num.astype(jnp.float32) * (2.0 * tok_here * blocks))
    lane_ids = jnp.arange(CAP, dtype=jnp.int32)
    own_count = counts[seq_here, block_here]
    own_start = offsets[seq_here, block_here]
    own_valid = lane_ids < own_count
    seq_list = jnp.concatenate([masked_pos[seq_here], jnp.zeros((CAP,), jnp.int32)])
    own_pos = lax.dynamic_slice_in_dim(seq_list, own_start, CAP) - block_here * tok_here
    own_pos = jnp.where(own_valid, own_pos, 0)
    own_rows = jnp.where(own_valid[:, None], hidden[own_pos].astype(jnp.float32), 0.0)
    squares = lax.psum(jnp.sum(own_rows * own_rows, axis=1), "vocab")
    inverse = lax.rsqrt(squares / model_width + EPSILON)
    normed_own = (own_rows * inverse[:, None] * norm_gain[None, :]).astype(jnp.bfloat16)
    normed_all = lax.all_gather(normed_own, "ctx", axis=0, tiled=True)
    row_ids = jnp.arange(ctx_count * CAP, dtype=jnp.int32)
    owner_ctx = row_ids // CAP
    lane_of = row_ids % CAP
    owner_seq = owner_ctx // blocks
    owner_block = owner_ctx % blocks
    row_valid = lane_of < counts[owner_seq, owner_block]
    list_slot = jnp.minimum(offsets[owner_seq, owner_block] + lane_of, slot_count - 1)
    row_targets = masked_targets[owner_seq, list_slot]
    row_factor = jnp.where(row_valid, weight[owner_seq], 0.0)
    row_total = normed_all.shape[0]
    rows_block = row_total // vocab_count
    logits = lax.psum_scatter(
        contract_last(normed_all, head), "vocab", scatter_dimension=0, tiled=True
    )
    block_start = vocab_index * rows_block
    target_cols = (
        lax.dynamic_slice_in_dim(row_targets, block_start, rows_block) - ctx_index * voc_here
    )
    factor = lax.dynamic_slice_in_dim(row_factor, block_start, rows_block)
    columns = jnp.arange(voc_here, dtype=jnp.int32)
    is_target = columns[None, :] == target_cols[:, None]
    picked = jnp.sum(jnp.where(is_target, logits, 0.0), axis=1)
    local_top = jnp.max(logits, axis=1)
    local_total = jnp.sum(jnp.exp(logits - local_top[:, None]), axis=1)
    row_top, exp_total, picked = joined((local_top, local_total, picked), "ctx", combine_stats)
    log_total = row_top + jnp.log(exp_total)
    loss_value = lax.psum(jnp.sum(factor * (log_total - picked)), "vocab")
    softmax_out = jnp.exp(logits - log_total[:, None])
    dlogits = (
        (LOSS_SCALE * factor)[:, None] * (softmax_out - is_target.astype(jnp.float32))
    ).astype(jnp.bfloat16)
    all_grads = lax.all_gather(dlogits, "vocab", axis=0, tiled=True)
    grad_head = lax.dot_general(
        all_grads, normed_all, (((0,), (0,)), ((), ())), preferred_element_type=jnp.float32
    ).astype(jnp.bfloat16)
    own_grad = lax.psum_scatter(
        jnp.dot(all_grads, head, preferred_element_type=jnp.float32),
        "ctx",
        scatter_dimension=0,
        tiled=True,
    )
    own_grad = jnp.where(own_valid[:, None], own_grad, 0.0)
    grad_gain = lax.psum(jnp.sum(own_grad * own_rows * inverse[:, None], axis=0), "ctx")
    inner_mean = (
        lax.psum(jnp.sum(norm_gain[None, :] * own_grad * own_rows, axis=1), "vocab") / model_width
    )
    row_grads = (
        inverse[:, None] * norm_gain[None, :] * own_grad
        - own_rows * (inverse * inverse * inverse * inner_mean)[:, None]
    )
    write_rows = jnp.where(own_valid, own_pos, tok_here)
    grad_hidden = (
        jnp.zeros((tok_here, width_here), jnp.bfloat16)
        .at[write_rows]
        .set(row_grads.astype(jnp.bfloat16), mode="drop")
    )
    return (loss_value, grad_hidden, grad_head, grad_gain)


def solution(mesh):
    placed = (P("ctx", "vocab"), P("vocab"), P("ctx", "vocab"), P(), P(), P(), P())
    return jax.shard_map(
        on_device,
        mesh=mesh,
        in_specs=placed,
        out_specs=(P(), P("ctx", "vocab"), P("ctx", "vocab"), P("vocab")),
        check_vma=False,
    )
```

profile of v0, /device:TPU:0, one launch (start us, length us, event | category | flops | bytes accessed | tf_op | source)
XLA Modules:
  0.0 292.8 jit_solution(3344552635716309176)
XLA Ops:
  7.2 0.0 all-gather.5.cloned.1.call-start
  7.3 0.8 and_select_fusion.4
  8.1 0.1 convert_reduce_fusion
  8.3 0.2 reduce_window_sum.11
  8.4 0.7 dynamic-slice_bitcast_fusion
  9.1 0.6 dynamic_slice.59
  9.7 0.6 dynamic_slice.61
  11.6 0.7 iota_compare_fusion.2
  12.9 0.7 compare_select_fusion
  13.7 0.6 gather_fusion.1
  14.3 0.2 multiply_reduce_fusion.2
  14.5 5.9 %psum.28 = f32[8]{0:T(128)S(1)} all-reduce(f32[8]{0:T(128)S(1)} %multiply_reduce_fusion.2), channel_id=1, replica_groups=mesh['ctx'=16,'vocab'=2] {'vocab'}, use_global_device_ids=true, to_apply=%region_3.4 | all-reduce | flops 8 | bytes 64 | tf_op jit(solution)/shard_map/psum | solution.py:59
  20.4 1.4 multiply_convert_fusion.1
  21.8 0.0 all-gather.5.cloned.1.call-update
  21.8 0.0 reduce-scatter.3.cloned.1.call-start
  21.9 39.7 %all-gather.5.cloned.1.call-done = bf16[128,4096]{1,0:T(8,128)(2,1)} async-done(((bf16[8,4096]{1,0:T(8,128)(2,1)}), bf16[128,4096]{1,0:T(8,128)(2,1)}) %all-gather.5.cloned.1.call-update) | async-done | bytes 1048592 | tf_op jit(solution)/shard_map/all_gather | solution.py:62
  61.6 7.1 %fusion.28 = f32[128,988]{1,0:T(8,128)} fusion(bf16[128,4096]{1,0:T(8,128)(2,1)} %all-gather.5.cloned.1.call-done, bf16[988,4096]{1,0:T(8,128)(2,1)} %param.11), kind=kOutput, calls=%fused_computation.82 | convolution fusion | flops 1035993088 | bytes 9648128 | tf_op jit(solution)/shard_map/dot_general | solution.py:23
  68.7 0.0 reduce-scatter.3.cloned.1.call-update
  68.7 0.0 reduce-scatter.5.cloned.1.call-start
  68.8 1.5 gather_fusion.2
  70.3 1.5 gather_fusion
  71.9 1.5 gather_fusion.3
  73.4 0.6 dynamic-slice
  74.6 0.1 dynamic-slice_subtract_fusion
  74.7 0.6 fusion.27
  75.3 1.3 compare_select_fusion.6
  76.6 5.8 %reduce-scatter.3.cloned.1.call-done = f32[64,988]{1,0:T(8,128)} async-done(((f32[128,988]{1,0:T(8,128)}), f32[64,988]{1,0:T(8,128)}) %reduce-scatter.3.cloned.1.call-update) | async-done | bytes 252944 | tf_op jit(solution)/shard_map/reduce_scatter | solution.py:74
  82.4 1.1 reduce_max.9
  83.5 0.2 dynamic-update-slice
  83.8 1.2 select_reduce_fusion
  85.0 0.2 dynamic-update-slice.2
  85.2 0.2 dynamic-update-slice.1
  85.4 61.0 %all-reduce.4 = (f32[1024]{0:T(1024)S(1)}, f32[1024]{0:T(1024)S(1)}, f32[1024]{0:T(1024)S(1)}) all-reduce(f32[1024]{0:T(1024)S(1)} %dynamic-update-slice, f32[1024]{0:T(1024)S(1)} %dynamic-update-slice.1, f32[1024]{0:T(1024)S(1)} %dynamic-update-slice.2), channel_id=2, replica_groups=mesh['ctx'=16,'vocab'=2] {'ctx'}, use_global_device_ids=true, to_apply=%add.1 | all-reduce | flops 3072 | bytes 24576
  146.4 0.1 reshape.215
  146.5 0.1 reshape.216
  146.6 0.1 reshape.217
  146.6 0.7 while.19
  147.3 0.7 multiply_reduce_fusion.3
  148.0 1.1 multiply_convert_fusion
  149.1 5.6 %all_gather.31 = bf16[128,988]{1,0:T(8,128)(2,1)S(1)} all-gather(bf16[64,988]{1,0:T(8,128)(2,1)S(1)} %multiply_convert_fusion), channel_id=1, replica_groups=mesh['ctx'=16,'vocab'=2] {'vocab'}, dimensions={0}, use_global_device_ids=true | all-gather | bytes 379392 | tf_op jit(solution)/shard_map/all_gather | solution.py:94
  154.8 6.0 %fusion.29 = f32[128,4096]{1,0:T(8,128)} fusion(bf16[128,988]{1,0:T(8,128)(2,1)S(1)} %all_gather.31, bf16[988,4096]{1,0:T(8,128)(2,1)} %param.11), kind=kOutput, calls=%fused_computation.83 | convolution fusion | flops 1035993088 | bytes 10443776 | tf_op jit(solution)/shard_map/dot_general | solution.py:99
  160.8 0.0 reduce-scatter.5.cloned.1.call-update
  160.8 5.6 %convolution_convert_fusion = bf16[988,4096]{1,0:T(8,128)(2,1)} fusion(bf16[128,988]{1,0:T(8,128)(2,1)S(1)} %all_gather.31, bf16[128,4096]{1,0:T(8,128)(2,1)S(1)} %copy-done.2), kind=kOutput, calls=%fused_computation.15 | convolution fusion | flops 1040039936 | bytes 9395200 | tf_op jit(solution)/shard_map/dot_general | solution.py:95
  166.4 52.7 %reduce-scatter.5.cloned.1.call-done = f32[8,4096]{1,0:T(8,128)} async-done(((f32[128,4096]{1,0:T(8,128)}), f32[8,4096]{1,0:T(8,128)}) %reduce-scatter.5.cloned.1.call-update) | async-done | bytes 131088 | tf_op jit(solution)/shard_map/reduce_scatter | solution.py:98
  219.1 1.2 multiply_reduce_fusion
  220.2 5.6 %all-reduce.5 = (f32[]{:T(128)}, f32[8]{0:T(128)S(1)}) all-reduce(f32[]{:T(128)} %get-tuple-element.212, f32[8]{0:T(128)S(1)} %get-tuple-element.188), channel_id=1, replica_groups=mesh['ctx'=16,'vocab'=2] {'vocab'}, use_global_device_ids=true, to_apply=%region_11.12 | all-reduce | flops 9 | bytes 72 | tf_op jit(solution)/shard_map/psum | solution.py:89
  225.8 57.6 %psum.31 = f32[4096]{0:T(1024)} all-reduce(f32[4096]{0:T(1024)S(1)} %get-tuple-element.187), channel_id=1, replica_groups=mesh['ctx'=16,'vocab'=2] {'ctx'}, use_global_device_ids=true, to_apply=%region_17.18 | all-reduce | flops 4096 | bytes 32768 | tf_op jit(solution)/shard_map/psum | solution.py:105
  283.4 2.9 scatter_custom_fusion
  (43 shorter events, 0.6 us)
Async XLA Ops:
  7.2 6.5 %copy-start = (bf16[256,4096]{1,0:T(8,128)(2,1)S(1)}, bf16[256,4096]{1,0:T(8,128)(2,1)}, u32[]{:S(2)}) copy-start(bf16[256,4096]{1,0:T(8,128)(2,1)} %param.9) | copy-start | bytes 6291460
  7.2 66.2 %copy-start.6 = (u32[32]{0:T(128)S(1)}, u32[32]{0:T(128)}, u32[]{:S(2)}) copy-start(u32[32]{0:T(128)} %constant.218) | copy-start | bytes 388
  7.2 64.7 %copy-start.1 = (s32[2,16]{1,0:T(2,128)S(1)}, s32[2,16]{1,0:T(2,128)}, u32[]{:S(2)}) copy-start(s32[2,16]{1,0:T(2,128)} %param.13) | copy-start | bytes 388
  7.2 67.5 %copy-start.4 = (s32[2]{0:T(128)S(1)}, s32[2]{0:T(128)}, u32[]{:S(2)}) copy-start(s32[2]{0:T(128)} %param.14) | copy-start | bytes 28
  7.2 67.5 %copy-start.5 = (s32[2]{0:T(128)S(1)}, s32[2]{0:T(128)}, u32[]{:S(2)}) copy-start(s32[2]{0:T(128)} %param.15) | copy-start | bytes 28
  7.2 54.4 %all-gather.5.cloned.1.call-start = ((), (), s32[]{:S(2)}) async-start(), calls=%async_computation.2 | async-start | bytes 1114112 | tf_op jit(solution)/shard_map/all_gather | solution.py:62
  21.8 60.6 %reduce-scatter.3.cloned.1.call-start = ((), (), s32[]{:S(2)}) async-start(), calls=%async_computation.3 | async-start | bytes 786432 | tf_op jit(solution)/shard_map/reduce_scatter | solution.py:74
  68.7 150.4 %reduce-scatter.5.cloned.1.call-start = ((), (), s32[]{:S(2)}) async-start(), calls=%async_computation.4 | async-start | bytes 2228224 | tf_op jit(solution)/shard_map/reduce_scatter | solution.py:98
  154.8 6.0 %copy-start.2 = (bf16[128,4096]{1,0:T(8,128)(2,1)S(1)}, bf16[128,4096]{1,0:T(8,128)(2,1)}, u32[]{:S(2)}) copy-start(bf16[128,4096]{1,0:T(8,128)(2,1)} %all-gather.5.cloned.1.call-done) | copy-start | bytes 3145732
  160.8 58.3 %copy-start.3 = (f32[4096]{0:T(1024)S(1)}, f32[4096]{0:T(1024)}, u32[]{:S(2)}) copy-start(f32[4096]{0:T(1024)} %param.10) | copy-start | bytes 49156
Sparse Core Ops, SparseCore 0:
  22.0 39.5 all-gather.4
  68.8 13.5 reduce-scatter.2
  160.9 58.1 reduce-scatter.4
where the time goes:
time: 293 us
  blocking collectives  136 us (46%)
  waiting for transfers between devices  98.2 us (34%)
  matrix products  18.7 us (6%)
  between operations  16.6 us (6%)
  other arithmetic  14.1 us (5%)
  local copies, waits for them, and re-layouts  9.14 us (3%)
    unnamed x1, blocking collectives  61 us
    psum x1, blocking collectives, on_device(): lax.psum(jnp.sum(own_grad * own_rows * inverse[:, None], axis=0), 'ctx')  57.6 us
    reduce_scatter x1, waiting for transfers between devices, on_device(): lax.psum_scatter(jnp.dot(all_grads, head, preferred_element_type=jnp.floa...  52.7 us
    all_gather x1, waiting for transfers between devices, on_device(): normed_all = lax.all_gather(normed_own, 'ctx', axis=0, tiled=True)  39.7 us
    dot_general x1, matrix products, contract_last(): lax.dot_general(left, right, (((1,), (1,)), ((), ())), preferred_element_...  7.06 us
    dot_general x1, matrix products, on_device(): jnp.dot(all_grads, head, preferred_element_type=jnp.float32)  5.98 us
    psum x1, blocking collectives, on_device(): squares = lax.psum(jnp.sum(own_rows * own_rows, axis=1), 'vocab')  5.89 us
  transfers between devices with their start and end apart: 3, of which 3 were waited for; matrix products, arithmetic and copies ran while one was open for 4% of the time, Pallas kernels for 0%

commit v1 on v0

--- a/solution.py
+++ b/solution.py
@@ -59,7 +59,12 @@
     squares = lax.psum(jnp.sum(own_rows * own_rows, axis=1), "vocab")
     inverse = lax.rsqrt(squares / model_width + EPSILON)
     normed_own = (own_rows * inverse[:, None] * norm_gain[None, :]).astype(jnp.bfloat16)
-    normed_all = lax.all_gather(normed_own, "ctx", axis=0, tiled=True)
+    ring = [normed_own]
+    for hop in range(15):
+        ring.append(lax.ppermute(ring[-1], "ctx", [(dev, (dev + 1) % 16) for dev in range(16)]))
+    normed_all = jnp.roll(
+        jnp.concatenate(ring[::-1], axis=0), (lax.axis_index("ctx") + 1) * ring[0].shape[0], axis=0
+    )
     row_ids = jnp.arange(ctx_count * CAP, dtype=jnp.int32)
     owner_ctx = row_ids // CAP
     lane_of = row_ids % CAP

time: 293 us -> 350 us (1.19)
  waiting for transfers between devices: 98.2 us -> 152 us
    ppermute x0 -> x15, waiting for transfers between devices: none -> 95.8 us  [on_device(): lax.ppermute(ring[-1], 'ctx', [(dev, (dev + 1) % 16) for dev in range(16)])]
    all_gather x1 -> x0, waiting for transfers between devices: 39.7 us -> none  [on_device(): normed_all = lax.all_gather(normed_own, 'ctx', axis=0, tiled=True)]
  transfers between devices with their start and end apart: 3 -> 17, of which waited for: 3 -> 17; matrix products, arithmetic and copies ran while one was open for 4% -> 4% of each run, Pallas kernels for 0% -> 0%
where the time goes in v1:
time: 350 us; the launch traced here: 349 us
  waiting for transfers between devices  152 us (43%)
  blocking collectives  136 us (39%)
  matrix products  19.5 us (6%)
  between operations  17.1 us (5%)
  other arithmetic  13.6 us (4%)
  local copies, waits for them, and re-layouts  10.7 us (3%)
    ppermute x15, waiting for transfers between devices, on_device(): lax.ppermute(ring[-1], 'ctx', [(dev, (dev + 1) % 16) for dev in range(16)])  95.8 us
    unnamed x1, blocking collectives  61.1 us
    psum x1, blocking collectives, on_device(): lax.psum(jnp.sum(own_grad * own_rows * inverse[:, None], axis=0), 'ctx')  57.6 us
    reduce_scatter x1, waiting for transfers between devices, on_device(): lax.psum_scatter(jnp.dot(all_grads, head, preferred_element_type=jnp.floa...  51.3 us
  transfers between devices with their start and end apart: 17, of which 17 were waited for; matrix products, arithmetic and copies ran while one was open for 4% of the time, Pallas kernels for 0%

profile of v1, /device:TPU:0, one launch (start us, length us, event | category | flops | bytes accessed | tf_op | source)
XLA Modules:
  0.0 349.0 jit_solution(2692927793039947385)
XLA Ops:
  7.3 0.8 and_select_fusion.4
  8.4 0.7 dynamic-slice_bitcast_fusion
  9.1 0.6 dynamic_slice.63
  9.7 0.6 dynamic_slice.65
  11.6 0.7 iota_compare_fusion.2
  12.9 0.7 compare_select_fusion
  13.6 0.6 gather_fusion.1
  14.4 5.9 %psum.28 = f32[8]{0:T(128)S(1)} all-reduce(f32[8]{0:T(128)S(1)} %multiply_reduce_fusion.2), channel_id=1, replica_groups=mesh['ctx'=16,'vocab'=2] {'vocab'}, use_global_device_ids=true, to_apply=%region_3.4 | all-reduce | flops 8 | bytes 64 | tf_op jit(solution)/shard_map/psum | solution.py:59
  20.3 0.8 multiply_convert_fusion.1
  21.2 6.4 %collective-permute-done = bf16[8,4096]{1,0:T(8,128)(2,1)S(1)} collective-permute-done((bf16[8,4096]{1,0:T(8,128)(2,1)S(1)}, bf16[8,4096]{1,0:T(8,128)(2,1)S(1)}, u32[]{:S(2)}, u32[]{:S(2)}) %collective-permute-start) | collective-permute-done | bytes 65568 | tf_op jit(solution)/shard_map/ppermute | solution.py:64
  27.6 6.4 %collective-permute-done.1 = bf16[8,4096]{1,0:T(8,128)(2,1)S(1)} collective-permute-done((bf16[8,4096]{1,0:T(8,128)(2,1)S(1)}, bf16[8,4096]{1,0:T(8,128)(2,1)S(1)}, u32[]{:S(2)}, u32[]{:S(2)}) %collective-permute-start.1) | collective-permute-done | bytes 65568 | tf_op jit(solution)/shard_map/ppermute | solution.py:64
  34.0 6.4 %collective-permute-done.2 = bf16[8,4096]{1,0:T(8,128)(2,1)S(1)} collective-permute-done((bf16[8,4096]{1,0:T(8,128)(2,1)S(1)}, bf16[8,4096]{1,0:T(8,128)(2,1)S(1)}, u32[]{:S(2)}, u32[]{:S(2)}) %collective-permute-start.2) | collective-permute-done | bytes 65568 | tf_op jit(solution)/shard_map/ppermute | solution.py:64
  40.4 6.4 %collective-permute-done.3 = bf16[8,4096]{1,0:T(8,128)(2,1)S(1)} collective-permute-done((bf16[8,4096]{1,0:T(8,128)(2,1)S(1)}, bf16[8,4096]{1,0:T(8,128)(2,1)S(1)}, u32[]{:S(2)}, u32[]{:S(2)}) %collective-permute-start.3) | collective-permute-done | bytes 65568 | tf_op jit(solution)/shard_map/ppermute | solution.py:64
  46.8 6.4 %collective-permute-done.4 = bf16[8,4096]{1,0:T(8,128)(2,1)S(1)} collective-permute-done((bf16[8,4096]{1,0:T(8,128)(2,1)S(1)}, bf16[8,4096]{1,0:T(8,128)(2,1)S(1)}, u32[]{:S(2)}, u32[]{:S(2)}) %collective-permute-start.4) | collective-permute-done | bytes 65568 | tf_op jit(solution)/shard_map/ppermute | solution.py:64
  53.2 6.4 %collective-permute-done.5 = bf16[8,4096]{1,0:T(8,128)(2,1)S(1)} collective-permute-done((bf16[8,4096]{1,0:T(8,128)(2,1)S(1)}, bf16[8,4096]{1,0:T(8,128)(2,1)S(1)}, u32[]{:S(2)}, u32[]{:S(2)}) %collective-permute-start.5) | collective-permute-done | bytes 65568 | tf_op jit(solution)/shard_map/ppermute | solution.py:64
  59.5 6.4 %collective-permute-done.6 = bf16[8,4096]{1,0:T(8,128)(2,1)S(1)} collective-permute-done((bf16[8,4096]{1,0:T(8,128)(2,1)S(1)}, bf16[8,4096]{1,0:T(8,128)(2,1)S(1)}, u32[]{:S(2)}, u32[]{:S(2)}) %collective-permute-start.6) | collective-permute-done | bytes 65568 | tf_op jit(solution)/shard_map/ppermute | solution.py:64
  65.9 6.4 %collective-permute-done.7 = bf16[8,4096]{1,0:T(8,128)(2,1)S(1)} collective-permute-done((bf16[8,4096]{1,0:T(8,128)(2,1)S(1)}, bf16[8,4096]{1,0:T(8,128)(2,1)S(1)}, u32[]{:S(2)}, u32[]{:S(2)}) %collective-permute-start.7) | collective-permute-done | bytes 65568 | tf_op jit(solution)/shard_map/ppermute | solution.py:64
  72.3 6.4 %collective-permute-done.8 = bf16[8,4096]{1,0:T(8,128)(2,1)S(1)} collective-permute-done((bf16[8,4096]{1,0:T(8,128)(2,1)S(1)}, bf16[8,4096]{1,0:T(8,128)(2,1)S(1)}, u32[]{:S(2)}, u32[]{:S(2)}) %collective-permute-start.8) | collective-permute-done | bytes 65568 | tf_op jit(solution)/shard_map/ppermute | solution.py:64
  78.7 6.4 %collective-permute-done.9 = bf16[8,4096]{1,0:T(8,128)(2,1)S(1)} collective-permute-done((bf16[8,4096]{1,0:T(8,128)(2,1)S(1)}, bf16[8,4096]{1,0:T(8,128)(2,1)S(1)}, u32[]{:S(2)}, u32[]{:S(2)}) %collective-permute-start.9) | collective-permute-done | bytes 65568 | tf_op jit(solution)/shard_map/ppermute | solution.py:64
  85.1 6.4 %collective-permute-done.10 = bf16[8,4096]{1,0:T(8,128)(2,1)S(1)} collective-permute-done((bf16[8,4096]{1,0:T(8,128)(2,1)S(1)}, bf16[8,4096]{1,0:T(8,128)(2,1)S(1)}, u32[]{:S(2)}, u32[]{:S(2)}) %collective-permute-start.10) | collective-permute-done | bytes 65568 | tf_op jit(solution)/shard_map/ppermute | solution.py:64
  91.5 6.4 %collective-permute-done.11 = bf16[8,4096]{1,0:T(8,128)(2,1)S(1)} collective-permute-done((bf16[8,4096]{1,0:T(8,128)(2,1)S(1)}, bf16[8,4096]{1,0:T(8,128)(2,1)S(1)}, u32[]{:S(2)}, u32[]{:S(2)}) %collective-permute-start.11) | collective-permute-done | bytes 65568 | tf_op jit(solution)/shard_map/ppermute | solution.py:64
  97.9 6.4 %collective-permute-done.12 = bf16[8,4096]{1,0:T(8,128)(2,1)S(1)} collective-permute-done((bf16[8,4096]{1,0:T(8,128)(2,1)S(1)}, bf16[8,4096]{1,0:T(8,128)(2,1)S(1)}, u32[]{:S(2)}, u32[]{:S(2)}) %collective-permute-start.12) | collective-permute-done | bytes 65568 | tf_op jit(solution)/shard_map/ppermute | solution.py:64
  104.3 6.4 %collective-permute-done.13 = bf16[8,4096]{1,0:T(8,128)(2,1)S(1)} collective-permute-done((bf16[8,4096]{1,0:T(8,128)(2,1)S(1)}, bf16[8,4096]{1,0:T(8,128)(2,1)S(1)}, u32[]{:S(2)}, u32[]{:S(2)}) %collective-permute-start.13) | collective-permute-done | bytes 65568 | tf_op jit(solution)/shard_map/ppermute | solution.py:64
  110.7 6.4 %collective-permute-done.14 = bf16[8,4096]{1,0:T(8,128)(2,1)S(1)} collective-permute-done((bf16[8,4096]{1,0:T(8,128)(2,1)S(1)}, bf16[8,4096]{1,0:T(8,128)(2,1)S(1)}, u32[]{:S(2)}, u32[]{:S(2)}) %collective-permute-start.14) | collective-permute-done | bytes 65568 | tf_op jit(solution)/shard_map/ppermute | solution.py:64
  117.7 1.3 copy-done.2
  119.0 6.7 %fusion.10 = f32[128,988]{1,0:T(8,128)} fusion(bf16[988,4096]{1,0:T(8,128)(2,1)} %param.11, bf16[256,4096]{1,0:T(8,128)(2,1)S(1)} %constant_dynamic-update-slice_fusion, s32[]{:T(128)S(6)} %select_n.206), kind=kOutput, calls=%fused_computation.19 | convolution fusion | flops 1035993088 | bytes 9648132 | tf_op jit(solution)/shard_map/dot_general | solution.py:23
  125.9 1.5 gather_fusion.2
  127.4 1.5 gather_fusion
  129.0 1.5 gather_fusion.3
  130.5 0.6 dynamic-slice
  131.8 0.6 fusion.32
  132.4 1.2 compare_select_fusion.6
  133.7 4.7 %reduce-scatter.3.cloned.1.call-done = f32[64,988]{1,0:T(8,128)} async-done(((f32[128,988]{1,0:T(8,128)}), f32[64,988]{1,0:T(8,128)}) %reduce-scatter.3.cloned.1.call-update) | async-done | bytes 252944 | tf_op jit(solution)/shard_map/reduce_scatter | solution.py:79
  138.4 1.1 reduce_max.9
  139.7 1.2 select_reduce_fusion
  140.9 0.2 dynamic-update-slice.2
  141.4 61.1 %all-reduce.4 = (f32[1024]{0:T(1024)S(1)}, f32[1024]{0:T(1024)S(1)}, f32[1024]{0:T(1024)S(1)}) all-reduce(f32[1024]{0:T(1024)S(1)} %dynamic-update-slice, f32[1024]{0:T(1024)S(1)} %dynamic-update-slice.1, f32[1024]{0:T(1024)S(1)} %dynamic-update-slice.2), channel_id=2, replica_groups=mesh['ctx'=16,'vocab'=2] {'ctx'}, use_global_device_ids=true, to_apply=%add.1 | all-reduce | flops 3072 | bytes 24576
  202.7 0.7 while.19
  203.4 0.7 multiply_reduce_fusion.3
  204.0 1.1 multiply_convert_fusion
  205.2 5.6 %all_gather.27 = bf16[128,988]{1,0:T(8,128)(2,1)S(1)} all-gather(bf16[64,988]{1,0:T(8,128)(2,1)S(1)} %multiply_convert_fusion), channel_id=1, replica_groups=mesh['ctx'=16,'vocab'=2] {'vocab'}, dimensions={0}, use_global_device_ids=true | all-gather | bytes 379392 | tf_op jit(solution)/shard_map/all_gather | solution.py:99
  210.8 5.9 %fusion.33 = f32[128,4096]{1,0:T(8,128)} fusion(bf16[128,988]{1,0:T(8,128)(2,1)S(1)} %all_gather.27, bf16[988,4096]{1,0:T(8,128)(2,1)} %param.11), kind=kOutput, calls=%fused_computation.119 | convolution fusion | flops 1035993088 | bytes 10443776 | tf_op jit(solution)/shard_map/dot_general | solution.py:104
  216.7 6.8 %convolution_convert_fusion = bf16[988,4096]{1,0:T(8,128)(2,1)} fusion(bf16[128,988]{1,0:T(8,128)(2,1)S(1)} %all_gather.27, bf16[256,4096]{1,0:T(8,128)(2,1)} %copy-done.2, s32[]{:T(128)S(6)} %select_n.206), kind=kOutput, calls=%fused_computation.15 | convolution fusion | flops 1040039936 | bytes 9395204 | tf_op jit(solution)/shard_map/dot_general | solution.py:100
  223.6 51.3 %reduce-scatter.5.cloned.1.call-done = f32[8,4096]{1,0:T(8,128)} async-done(((f32[128,4096]{1,0:T(8,128)}), f32[8,4096]{1,0:T(8,128)}) %reduce-scatter.5.cloned.1.call-update) | async-done | bytes 131088 | tf_op jit(solution)/shard_map/reduce_scatter | solution.py:103
  274.9 1.1 multiply_reduce_fusion
  276.0 5.6 %all-reduce.5 = (f32[]{:T(128)}, f32[8]{0:T(128)S(1)}) all-reduce(f32[]{:T(128)} %get-tuple-element.212, f32[8]{0:T(128)S(1)} %get-tuple-element.188), channel_id=1, replica_groups=mesh['ctx'=16,'vocab'=2] {'vocab'}, use_global_device_ids=true, to_apply=%region_11.12 | all-reduce | flops 9 | bytes 72 | tf_op jit(solution)/shard_map/psum | solution.py:94
  281.6 57.6 %psum.31 = f32[4096]{0:T(1024)} all-reduce(f32[4096]{0:T(1024)S(1)} %get-tuple-element.187), channel_id=1, replica_groups=mesh['ctx'=16,'vocab'=2] {'ctx'}, use_global_device_ids=true, to_apply=%region_17.18 | all-reduce | flops 4096 | bytes 32768 | tf_op jit(solution)/shard_map/psum | solution.py:110
  339.2 2.9 scatter_custom_fusion
  (102 shorter events, 2.4 us)
Async XLA Ops:
  7.2 6.5 %copy-start = (bf16[256,4096]{1,0:T(8,128)(2,1)S(1)}, bf16[256,4096]{1,0:T(8,128)(2,1)}, u32[]{:S(2)}) copy-start(bf16[256,4096]{1,0:T(8,128)(2,1)} %param.9) | copy-start | bytes 6291460
  7.2 110.1 %copy-start.3 = (f32[4096]{0:T(1024)S(1)}, f32[4096]{0:T(1024)}, u32[]{:S(2)}) copy-start(f32[4096]{0:T(1024)} %param.10) | copy-start | bytes 49156
  7.2 131.2 %reduce-scatter.3.cloned.1.call-start = ((), (), s32[]{:S(2)}) async-start(), calls=%async_computation.2 | async-start | bytes 786432 | tf_op jit(solution)/shard_map/reduce_scatter | solution.py:79
  21.2 6.4 %collective-permute-start = (bf16[8,4096]{1,0:T(8,128)(2,1)S(1)}, bf16[8,4096]{1,0:T(8,128)(2,1)S(1)}, u32[]{:S(2)}, u32[]{:S(2)}) collective-permute-start(bf16[8,4096]{1,0:T(8,128)(2,1)S(1)} %multiply_convert_fusion.1), channel_id=1, source_target_pairs={{0,2},{2,4},{4,6},{6,8},{8,10},{10,12},{12,14},{14,16},{16,18},{18... | collective-permute-start | bytes 196616 | tf_op jit(solution)/shard_map/ppermute | solution.py:64
  27.6 6.4 %collective-permute-start.1 = (bf16[8,4096]{1,0:T(8,128)(2,1)S(1)}, bf16[8,4096]{1,0:T(8,128)(2,1)S(1)}, u32[]{:S(2)}, u32[]{:S(2)}) collective-permute-start(bf16[8,4096]{1,0:T(8,128)(2,1)S(1)} %collective-permute-done), channel_id=1, source_target_pairs={{0,2},{2,4},{4,6},{6,8},{8,10},{10,12},{12,14},{14,16},{16,18},{18... | collective-permute-start | bytes 196616 | tf_op jit(solution)/shard_map/ppermute | solution.py:64
  34.0 6.4 %collective-permute-start.2 = (bf16[8,4096]{1,0:T(8,128)(2,1)S(1)}, bf16[8,4096]{1,0:T(8,128)(2,1)S(1)}, u32[]{:S(2)}, u32[]{:S(2)}) collective-permute-start(bf16[8,4096]{1,0:T(8,128)(2,1)S(1)} %collective-permute-done.1), channel_id=1, source_target_pairs={{0,2},{2,4},{4,6},{6,8},{8,10},{10,12},{12,14},{14,16},{16,18},{18... | collective-permute-start | bytes 196616 | tf_op jit(solution)/shard_map/ppermute | solution.py:64
  40.4 6.4 %collective-permute-start.3 = (bf16[8,4096]{1,0:T(8,128)(2,1)S(1)}, bf16[8,4096]{1,0:T(8,128)(2,1)S(1)}, u32[]{:S(2)}, u32[]{:S(2)}) collective-permute-start(bf16[8,4096]{1,0:T(8,128)(2,1)S(1)} %collective-permute-done.2), channel_id=1, source_target_pairs={{0,2},{2,4},{4,6},{6,8},{8,10},{10,12},{12,14},{14,16},{16,18},{18... | collective-permute-start | bytes 196616 | tf_op jit(solution)/shard_map/ppermute | solution.py:64
  46.8 6.4 %collective-permute-start.4 = (bf16[8,4096]{1,0:T(8,128)(2,1)S(1)}, bf16[8,4096]{1,0:T(8,128)(2,1)S(1)}, u32[]{:S(2)}, u32[]{:S(2)}) collective-permute-start(bf16[8,4096]{1,0:T(8,128)(2,1)S(1)} %collective-permute-done.3), channel_id=1, source_target_pairs={{0,2},{2,4},{4,6},{6,8},{8,10},{10,12},{12,14},{14,16},{16,18},{18... | collective-permute-start | bytes 196616 | tf_op jit(solution)/shard_map/ppermute | solution.py:64
  53.2 6.4 %collective-permute-start.5 = (bf16[8,4096]{1,0:T(8,128)(2,1)S(1)}, bf16[8,4096]{1,0:T(8,128)(2,1)S(1)}, u32[]{:S(2)}, u32[]{:S(2)}) collective-permute-start(bf16[8,4096]{1,0:T(8,128)(2,1)S(1)} %collective-permute-done.4), channel_id=1, source_target_pairs={{0,2},{2,4},{4,6},{6,8},{8,10},{10,12},{12,14},{14,16},{16,18},{18... | collective-permute-start | bytes 196616 | tf_op jit(solution)/shard_map/ppermute | solution.py:64
  59.5 6.4 %collective-permute-start.6 = (bf16[8,4096]{1,0:T(8,128)(2,1)S(1)}, bf16[8,4096]{1,0:T(8,128)(2,1)S(1)}, u32[]{:S(2)}, u32[]{:S(2)}) collective-permute-start(bf16[8,4096]{1,0:T(8,128)(2,1)S(1)} %collective-permute-done.5), channel_id=1, source_target_pairs={{0,2},{2,4},{4,6},{6,8},{8,10},{10,12},{12,14},{14,16},{16,18},{18... | collective-permute-start | bytes 196616 | tf_op jit(solution)/shard_map/ppermute | solution.py:64
  65.9 6.4 %collective-permute-start.7 = (bf16[8,4096]{1,0:T(8,128)(2,1)S(1)}, bf16[8,4096]{1,0:T(8,128)(2,1)S(1)}, u32[]{:S(2)}, u32[]{:S(2)}) collective-permute-start(bf16[8,4096]{1,0:T(8,128)(2,1)S(1)} %collective-permute-done.6), channel_id=1, source_target_pairs={{0,2},{2,4},{4,6},{6,8},{8,10},{10,12},{12,14},{14,16},{16,18},{18... | collective-permute-start | bytes 196616 | tf_op jit(solution)/shard_map/ppermute | solution.py:64
  72.3 6.4 %collective-permute-start.8 = (bf16[8,4096]{1,0:T(8,128)(2,1)S(1)}, bf16[8,4096]{1,0:T(8,128)(2,1)S(1)}, u32[]{:S(2)}, u32[]{:S(2)}) collective-permute-start(bf16[8,4096]{1,0:T(8,128)(2,1)S(1)} %collective-permute-done.7), channel_id=1, source_target_pairs={{0,2},{2,4},{4,6},{6,8},{8,10},{10,12},{12,14},{14,16},{16,18},{18... | collective-permute-start | bytes 196616 | tf_op jit(solution)/shard_map/ppermute | solution.py:64
  78.7 6.4 %collective-permute-start.9 = (bf16[8,4096]{1,0:T(8,128)(2,1)S(1)}, bf16[8,4096]{1,0:T(8,128)(2,1)S(1)}, u32[]{:S(2)}, u32[]{:S(2)}) collective-permute-start(bf16[8,4096]{1,0:T(8,128)(2,1)S(1)} %collective-permute-done.8), channel_id=1, source_target_pairs={{0,2},{2,4},{4,6},{6,8},{8,10},{10,12},{12,14},{14,16},{16,18},{18... | collective-permute-start | bytes 196616 | tf_op jit(solution)/shard_map/ppermute | solution.py:64
  85.1 6.4 %collective-permute-start.10 = (bf16[8,4096]{1,0:T(8,128)(2,1)S(1)}, bf16[8,4096]{1,0:T(8,128)(2,1)S(1)}, u32[]{:S(2)}, u32[]{:S(2)}) collective-permute-start(bf16[8,4096]{1,0:T(8,128)(2,1)S(1)} %collective-permute-done.9), channel_id=1, source_target_pairs={{0,2},{2,4},{4,6},{6,8},{8,10},{10,12},{12,14},{14,16},{16,18},{18... | collective-permute-start | bytes 196616 | tf_op jit(solution)/shard_map/ppermute | solution.py:64
  91.5 6.4 %collective-permute-start.11 = (bf16[8,4096]{1,0:T(8,128)(2,1)S(1)}, bf16[8,4096]{1,0:T(8,128)(2,1)S(1)}, u32[]{:S(2)}, u32[]{:S(2)}) collective-permute-start(bf16[8,4096]{1,0:T(8,128)(2,1)S(1)} %collective-permute-done.10), channel_id=1, source_target_pairs={{0,2},{2,4},{4,6},{6,8},{8,10},{10,12},{12,14},{14,16},{16,18},{18... | collective-permute-start | bytes 196616 | tf_op jit(solution)/shard_map/ppermute | solution.py:64
  97.9 6.4 %collective-permute-start.12 = (bf16[8,4096]{1,0:T(8,128)(2,1)S(1)}, bf16[8,4096]{1,0:T(8,128)(2,1)S(1)}, u32[]{:S(2)}, u32[]{:S(2)}) collective-permute-start(bf16[8,4096]{1,0:T(8,128)(2,1)S(1)} %collective-permute-done.11), channel_id=1, source_target_pairs={{0,2},{2,4},{4,6},{6,8},{8,10},{10,12},{12,14},{14,16},{16,18},{18... | collective-permute-start | bytes 196616 | tf_op jit(solution)/shard_map/ppermute | solution.py:64
  104.3 6.4 %collective-permute-start.13 = (bf16[8,4096]{1,0:T(8,128)(2,1)S(1)}, bf16[8,4096]{1,0:T(8,128)(2,1)S(1)}, u32[]{:S(2)}, u32[]{:S(2)}) collective-permute-start(bf16[8,4096]{1,0:T(8,128)(2,1)S(1)} %collective-permute-done.12), channel_id=1, source_target_pairs={{0,2},{2,4},{4,6},{6,8},{8,10},{10,12},{12,14},{14,16},{16,18},{18... | collective-permute-start | bytes 196616 | tf_op jit(solution)/shard_map/ppermute | solution.py:64
  110.6 6.4 %collective-permute-start.14 = (bf16[8,4096]{1,0:T(8,128)(2,1)S(1)}, bf16[8,4096]{1,0:T(8,128)(2,1)S(1)}, u32[]{:S(2)}, u32[]{:S(2)}) collective-permute-start(bf16[8,4096]{1,0:T(8,128)(2,1)S(1)} %collective-permute-done.13), channel_id=1, source_target_pairs={{0,2},{2,4},{4,6},{6,8},{8,10},{10,12},{12,14},{14,16},{16,18},{18... | collective-permute-start | bytes 196616 | tf_op jit(solution)/shard_map/ppermute | solution.py:64
  117.7 1.4 copy-start.2
  119.0 9.9 %copy-start.1 = (s32[2,16]{1,0:T(2,128)S(1)}, s32[2,16]{1,0:T(2,128)}, u32[]{:S(2)}) copy-start(s32[2,16]{1,0:T(2,128)} %param.13) | copy-start | bytes 388
  125.8 4.7 %copy-start.6 = (u32[32]{0:T(128)S(1)}, u32[32]{0:T(128)}, u32[]{:S(2)}) copy-start(u32[32]{0:T(128)} %constant.238) | copy-start | bytes 388
  125.8 6.1 %copy-start.4 = (s32[2]{0:T(128)S(1)}, s32[2]{0:T(128)}, u32[]{:S(2)}) copy-start(s32[2]{0:T(128)} %param.14) | copy-start | bytes 28
  125.8 6.1 %copy-start.5 = (s32[2]{0:T(128)S(1)}, s32[2]{0:T(128)}, u32[]{:S(2)}) copy-start(s32[2]{0:T(128)} %param.15) | copy-start | bytes 28
  125.8 149.1 %reduce-scatter.5.cloned.1.call-start = ((), (), s32[]{:S(2)}) async-start(), calls=%async_computation.3 | async-start | bytes 2228224 | tf_op jit(solution)/shard_map/reduce_scatter | solution.py:103
Sparse Core Ops, SparseCore 0:
  125.9 12.4 reduce-scatter.2
  216.8 58.0 reduce-scatter.4
